TPU v7x, 32 devices: a whole 2x2x4 slice. The times are simulated.
32 devices in a mesh: tok: 4 (over z), hid: 8 (over y, x, core).
Axes of the slice: x: 2, y: 2, z: 4, core: 2. Of those that a mesh axis runs over, the one named last changes fastest.
Arguments:
- tokens: bfloat16 [2048, 1024], P('tok', 'hid'), may hold values from -6 to 6
- cotangent: bfloat16 [2048, 1024], P('tok', 'hid'), may hold values from -6 to 6
- frozen_in: bfloat16 [1024, 16384], P('tok', 'hid'), may hold values from -0.1875 to 0.1875
- frozen_out: bfloat16 [16384, 1024], P('hid', 'tok'), may hold values from -0.046875 to 0.046875
- input_adapter_first: bfloat16 [1024, 128], P('hid'), may hold values from -0.1875 to 0.1875
- input_adapter_second: bfloat16 [128, 16384], P(None, 'hid'), may hold values from -0.5 to 0.5
- adapter_out_a: bfloat16 [16384, 128], P('hid'), may hold values from -0.046875 to 0.046875
- adapter_out_b: bfloat16 [128, 1024], replicated, may hold values from -0.5 to 0.5
Outputs:
- input_gradient: float32 [2048, 1024], P('tok', 'hid')
- grad_in_a: float32 [1024, 128], P('hid')
- grad_in_b: float32 [128, 16384], P(None, 'hid')
- grad_out_a: float32 [16384, 128], P('hid')
- grad_out_b: float32 [128, 1024], P(None, 'hid')
All inputs are finite; a program needn't handle non-finite values.
Results may differ from a plain program's by a relative error of at most 0.0029.
Values may be sent and summed in bfloat16 or wider, within the bound.
A program may use at most 64 MiB of HBM per device.

v0:
```python
import math
import jax
import jax.numpy as jnp
from jax import lax
from jax.sharding import PartitionSpec as P

ADAPTER_SCALE = 0.5
GELU_K = 0.7978845608
GELU_C = 0.044715


def gelu_pair(pre_activation):
    tangent = jnp.tanh(
        GELU_K * (pre_activation + GELU_C * pre_activation * pre_activation * pre_activation)
    )
    value_out = 0.5 * pre_activation * (1.0 + tangent)
    slopes = 0.5 * (1.0 + tangent) + 0.5 * pre_activation * (1.0 - tangent * tangent) * GELU_K * (
        1.0 + 3.0 * GELU_C * pre_activation * pre_activation
    )
    return (value_out, slopes)


def local(
    tokens,
    cotangent,
    frozen_in,
    frozen_out,
    input_adapter_first,
    input_adapter_second,
    adapter_out_a,
    adapter_out_b,
):
    highest_precision = lax.Precision.HIGHEST
    device_local_rows = tokens.shape[0]
    rank_width = input_adapter_second.shape[0]
    gradient_scale = ADAPTER_SCALE / math.sqrt(device_local_rows * lax.axis_size("tok"))
    full_tokens, full_cotan = (
        lax.all_gather(tokens, "hid", axis=1, tiled=True),
        lax.all_gather(cotangent, "hid", axis=1, tiled=True),
    )
    in_rows = lax.all_gather(frozen_in, "tok", axis=0, tiled=True)
    in_a_full = lax.all_gather(input_adapter_first, "hid", axis=0, tiled=True)
    lowrank_input = jnp.dot(full_tokens, in_a_full, preferred_element_type=jnp.float32)
    second_float = input_adapter_second.astype(jnp.float32)
    out_a_float = adapter_out_a.astype(jnp.float32)
    pre_activation = jnp.dot(
        full_tokens, in_rows, preferred_element_type=jnp.float32
    ) + ADAPTER_SCALE * jnp.dot(lowrank_input, second_float, precision=highest_precision)
    value_out, slopes = gelu_pair(pre_activation)
    hidden_act = value_out.astype(jnp.bfloat16)
    backward_lowrank = jnp.einsum(
        "td,rd->tr", full_cotan, adapter_out_b, preferred_element_type=jnp.float32
    )
    rank_out = jnp.dot(hidden_act, adapter_out_a, preferred_element_type=jnp.float32)
    dense_backward = jnp.einsum(
        "td,fd->tf",
        full_cotan,
        lax.all_gather(frozen_out, "tok", axis=1, tiled=True),
        preferred_element_type=jnp.float32,
    )
    dense_backward = dense_backward + ADAPTER_SCALE * jnp.dot(
        backward_lowrank, out_a_float.T, precision=highest_precision
    )
    grad_pre = (dense_backward * slopes).astype(jnp.bfloat16)
    rank_backward = jnp.einsum(
        "tf,rf->tr", grad_pre, input_adapter_second, preferred_element_type=jnp.float32
    )
    dense_in = jnp.einsum("tf,df->td", grad_pre, in_rows, preferred_element_type=jnp.float32)
    grad_out_a = gradient_scale * jnp.dot(
        hidden_act.astype(jnp.float32).T, backward_lowrank, precision=highest_precision
    )
    grad_in_b = gradient_scale * jnp.dot(
        lowrank_input.T, grad_pre.astype(jnp.float32), precision=highest_precision
    )
    in_a_float = in_a_full.astype(jnp.float32)
    dx_term = dense_in + ADAPTER_SCALE * jnp.dot(
        rank_backward, in_a_float.T, precision=highest_precision
    )
    out_term = jnp.dot(rank_out.T, full_cotan.astype(jnp.float32), precision=highest_precision)
    in_term = jnp.dot(rank_backward.T, full_tokens.astype(jnp.float32), precision=highest_precision)
    rank_terms = jnp.concatenate([out_term, in_term], axis=0)
    input_gradient, rank_local = (
        lax.psum_scatter(dx_term, "hid", scatter_dimension=1, tiled=True),
        lax.psum_scatter(rank_terms, "hid", scatter_dimension=1, tiled=True),
    )
    grad_out_a, grad_in_b, rank_total = lax.psum((grad_out_a, grad_in_b, rank_local), "tok")
    grad_out_b = gradient_scale * rank_total[:rank_width]
    grad_in_a = gradient_scale * rank_total[rank_width:].T
    return (input_gradient, grad_in_a, grad_in_b, grad_out_a, grad_out_b)


def solution(mesh):
    in_specs = (
        P("tok", "hid"),
        P("tok", "hid"),
        P("tok", "hid"),
        P("hid", "tok"),
        P("hid", None),
        P(None, "hid"),
        P("hid", None),
        P(),
    )
    out_specs = (P("tok", "hid"), P("hid", None), P(None, "hid"), P("hid", None), P(None, "hid"))
    return jax.shard_map(local, mesh=mesh, in_specs=in_specs, out_specs=out_specs, check_vma=False)
```

profile of v0, /device:TPU:0, one launch (start us, length us, event | category | flops | bytes accessed | tf_op | source)
XLA Modules:
  0.0 421.3 jit_solution(1950593718763780741)
XLA Ops:
  7.2 0.0 copy-start
  7.2 0.0 all-gather.5.cloned.1.call-start
  7.2 0.7 all-gather.5.cloned.1.call-update
  7.9 0.0 all-gather.9.cloned.1.call-start
  8.0 0.7 all-gather.9.cloned.1.call-update
  8.7 0.0 all-gather.11.cloned.1.call-start
  8.7 0.7 all-gather.11.cloned.1.call-update
  9.4 0.0 all-gather.7.cloned.1.call-start
  9.4 0.5 all-gather.7.cloned.1.call-update
  10.0 0.0 reduce-scatter.5.cloned.1.call-start
  10.0 11.0 %all_gather.19 = bf16[1024,128]{1,0:T(8,128)(2,1)S(1)} all-gather(bf16[128,128]{1,0:T(8,128)(2,1)} %param.12), channel_id=1, replica_groups=mesh['tok'=4,'hid'=8] {'hid'}, dimensions={0}, use_global_device_ids=true | all-gather | bytes 294912 | tf_op jit(solution)/shard_map/all_gather | solution.py:42
  21.0 15.1 %all-gather.5.cloned.1.call-done = bf16[512,1024]{1,0:T(8,128)(2,1)} async-done(((bf16[512,128]{1,0:T(8,128)(2,1)}), bf16[512,1024]{1,0:T(8,128)(2,1)}) %all-gather.5.cloned.1.call-update) | async-done | bytes 1048592 | tf_op jit(solution)/shard_map/all_gather | solution.py:39
  36.1 1.7 fusion.9
  37.8 23.7 %all-gather.9.cloned.1.call-done = bf16[512,1024]{1,0:T(8,128)(2,1)} async-done(((bf16[512,128]{1,0:T(8,128)(2,1)}), bf16[512,1024]{1,0:T(8,128)(2,1)}) %all-gather.9.cloned.1.call-update) | async-done | bytes 1048592 | tf_op jit(solution)/shard_map/all_gather | solution.py:38
  61.5 1.7 fusion.11
  63.1 0.0 copy-start.6
  63.2 80.7 %all-gather.11.cloned.1.call-done = bf16[1024,2048]{1,0:T(8,128)(2,1)} async-done(((bf16[256,2048]{1,0:T(8,128)(2,1)}), bf16[1024,2048]{1,0:T(8,128)(2,1)}) %all-gather.11.cloned.1.call-update) | async-done | bytes 4194320 | tf_op jit(solution)/shard_map/all_gather | solution.py:41
  143.8 4.8 %fusion.10 = f32[512,2048]{1,0:T(8,128)S(1)} fusion(bf16[512,1024]{1,0:T(8,128)(2,1)} %all-gather.9.cloned.1.call-done, bf16[1024,2048]{1,0:T(8,128)(2,1)} %all-gather.11.cloned.1.call-done), kind=kOutput, calls=%fused_computation.20 | convolution fusion | flops 2147483648 | bytes 9437184 | tf_op jit(solution)/shard_map/dot_general | solution.py:46
  148.7 0.0 copy-done.6
  148.7 0.0 copy-done
  148.7 0.0 copy-start.3
  148.7 5.9 %multiply_convert_fusion = (bf16[512,2048]{1,0:T(8,128)(2,1)}, f32[512,2048]{1,0:T(8,128)}) fusion(f32[512,2048]{1,0:T(8,128)S(1)} %fusion.10, f32[512,128]{1,0:T(8,128)S(1)} %fusion.11, bf16[128,2048]{1,0:T(8,128)(2,1)S(1)} %copy-done), kind=kOutput, calls=%fused_computation.9 | convolution fusion | flops 1622147072 | bytes 11272192 | tf_op jit(solution)/shard_map/dot_general | solution.py:48
  154.6 69.7 %all-gather.7.cloned.1.call-done = bf16[2048,1024]{1,0:T(8,128)(2,1)} async-done(((bf16[2048,256]{1,0:T(8,128)(2,1)}), bf16[2048,1024]{1,0:T(8,128)(2,1)}) %all-gather.7.cloned.1.call-update) | async-done | bytes 4194320 | tf_op jit(solution)/shard_map/all_gather | solution.py:58
  224.3 0.0 copy-done.3
  224.3 4.7 %fusion.8 = f32[512,2048]{1,0:T(8,128)S(1)} fusion(bf16[512,1024]{1,0:T(8,128)(2,1)S(1)} %copy-done.3, bf16[2048,1024]{1,0:T(8,128)(2,1)} %all-gather.7.cloned.1.call-done), kind=kOutput, calls=%fused_computation.18 | convolution fusion | flops 2147483648 | bytes 9437184 | tf_op jit(solution)/shard_map/td,fd->tf/dot_general | solution.py:55
  229.0 0.0 copy-done.7
  229.1 5.1 %fusion.6 = bf16[512,2048]{1,0:T(8,128)(2,1)S(1)} fusion(f32[512,2048]{1,0:T(8,128)S(1)} %copy-done.8, f32[512,2048]{1,0:T(8,128)S(1)} %fusion.8, f32[512,128]{1,0:T(8,128)S(1)} %fusion.9, bf16[2048,128]{1,0:T(8,128)(2,1)S(1)} %copy-done.7), kind=kOutput, calls=%fused_computation.8 | convolution fusion | flops 1632632832 | bytes 11272192 | tf_op jit(solution)/shard_map/dot_general | solution.py:61
  234.1 0.7 fusion.13
  234.9 0.7 fusion.14
  235.6 0.7 fusion.16
  236.3 0.7 fusion.15
  236.9 1.1 pad_maximum_fusion
  238.0 0.0 reduce-scatter.5.cloned.1.call-update
  238.0 0.0 all-reduce.3.cloned.1.call-start
  238.1 3.1 convolution_multiply_fusion.1
  241.2 3.3 convolution_multiply_fusion
  244.5 27.9 %reduce-scatter.5.cloned.1.call-done = f32[256,128]{1,0:T(8,128)} async-done(((f32[256,1024]{1,0:T(8,128)}), f32[256,128]{1,0:T(8,128)}) %reduce-scatter.5.cloned.1.call-update) | async-done | bytes 131088 | tf_op jit(solution)/shard_map/reduce_scatter | solution.py:84
  272.4 0.0 all-reduce.3.cloned.1.call-update
  272.4 0.0 reduce-scatter.3.cloned.1.call-start
  272.4 4.5 %fusion.12 = f32[512,1024]{1,0:T(8,128)S(1)} fusion(bf16[512,2048]{1,0:T(8,128)(2,1)S(1)} %fusion.6, bf16[1024,2048]{1,0:T(8,128)(2,1)} %all-gather.11.cloned.1.call-done), kind=kOutput, calls=%fused_computation.22 | convolution fusion | flops 2147483648 | bytes 8388608 | tf_op jit(solution)/shard_map/tf,df->td/dot_general | solution.py:68
  277.0 2.4 multiply_add_fusion.2
  279.4 0.0 reduce-scatter.3.cloned.1.call-update
  279.4 86.5 %all-reduce.3.cloned.1.call-done = (f32[256,128]{1,0:T(8,128)}, f32[128,2048]{1,0:T(8,128)}, f32[2048,128]{1,0:T(8,128)}) async-done(((f32[256,128]{1,0:T(8,128)}, f32[128,2048]{1,0:T(8,128)}, f32[2048,128]{1,0:T(8,128)}), (f32[256,128]{1,0:T(8,128)}, f32[128,2048]{1,0:T(8,128)}, f32[2048,128]{1,0:T(8,128)})) %all-reduce.3.cloned.1.call-update) | async-done | bytes 2228240 | tf_op jit(solution)/shard_map/psum | solution.py:86
  365.8 1.5 slice_multiply_fusion
  367.4 0.7 copy.13
  368.1 41.8 %reduce-scatter.3.cloned.1.call-done = f32[512,128]{1,0:T(8,128)} async-done(((f32[512,1024]{1,0:T(8,128)}), f32[512,128]{1,0:T(8,128)}) %reduce-scatter.3.cloned.1.call-update) | async-done | bytes 262160 | tf_op jit(solution)/shard_map/reduce_scatter | solution.py:83
  409.9 2.3 copy.17
  412.2 2.3 copy.18
  (11 shorter events, 0.0 us)
Async XLA Ops:
  7.2 141.5 %copy-start = (bf16[128,2048]{1,0:T(8,128)(2,1)S(1)}, bf16[128,2048]{1,0:T(8,128)(2,1)}, u32[]{:S(2)}) copy-start(bf16[128,2048]{1,0:T(8,128)(2,1)} %param.13) | copy-start | bytes 1572868
  7.2 28.9 %all-gather.5.cloned.1.call-start = ((), (), s32[]{:S(2)}) async-start(), calls=%async_computation.2 | async-start | bytes 1179648 | tf_op jit(solution)/shard_map/all_gather | solution.py:39
  7.9 53.6 %all-gather.9.cloned.1.call-start = ((), (), s32[]{:S(2)}) async-start(), calls=%async_computation.4 | async-start | bytes 1179648 | tf_op jit(solution)/shard_map/all_gather | solution.py:38
  8.7 135.2 %all-gather.11.cloned.1.call-start = ((), (), s32[]{:S(2)}) async-start(), calls=%async_computation.5 | async-start | bytes 5242880 | tf_op jit(solution)/shard_map/all_gather | solution.py:41
  9.4 214.9 %all-gather.7.cloned.1.call-start = ((), (), s32[]{:S(2)}) async-start(), calls=%async_computation.3 | async-start | bytes 5242880 | tf_op jit(solution)/shard_map/all_gather | solution.py:58
  10.0 262.4 %reduce-scatter.5.cloned.1.call-start = ((), (), s32[]{:S(2)}) async-start(), calls=%async_computation.7 | async-start | bytes 1179648 | tf_op jit(solution)/shard_map/reduce_scatter | solution.py:84
  63.1 85.5 %copy-start.6 = (f32[512,128]{1,0:T(8,128)}, f32[512,128]{1,0:T(8,128)S(1)}, u32[]{:S(2)}) copy-start(f32[512,128]{1,0:T(8,128)S(1)} %fusion.11) | copy-start | bytes 786436
  148.7 75.6 %copy-start.3 = (bf16[512,1024]{1,0:T(8,128)(2,1)S(1)}, bf16[512,1024]{1,0:T(8,128)(2,1)}, u32[]{:S(2)}) copy-start(bf16[512,1024]{1,0:T(8,128)(2,1)} %all-gather.5.cloned.1.call-done) | copy-start | bytes 3145732
  224.3 4.7 %copy-start.7 = (bf16[2048,128]{1,0:T(8,128)(2,1)S(1)}, bf16[2048,128]{1,0:T(8,128)(2,1)}, u32[]{:S(2)}) copy-start(bf16[2048,128]{1,0:T(8,128)(2,1)} %param.14) | copy-start | bytes 1572868
  224.3 4.7 %copy-start.8 = (f32[512,2048]{1,0:T(8,128)S(1)}, f32[512,2048]{1,0:T(8,128)}, u32[]{:S(2)}) copy-start(f32[512,2048]{1,0:T(8,128)} %get-tuple-element.16) | copy-start | bytes 12582916
  229.0 5.8 %copy-start.1 = (bf16[512,2048]{1,0:T(8,128)(2,1)S(1)}, bf16[512,2048]{1,0:T(8,128)(2,1)}, u32[]{:S(2)}) copy-start(bf16[512,2048]{1,0:T(8,128)(2,1)} %get-tuple-element.15) | copy-start | bytes 6291460
  234.1 1.5 copy-start.5
  234.1 2.1 copy-start.4
  238.0 127.8 %all-reduce.3.cloned.1.call-start = ((), (), s32[]{:S(2)}) async-start(), calls=%async_computation.8 | async-start | bytes 4456448 | tf_op jit(solution)/shard_map/psum | solution.py:86
  238.1 3.1 copy-start.2
  272.4 137.5 %reduce-scatter.3.cloned.1.call-start = ((), (), s32[]{:S(2)}) async-start(), calls=%async_computation.6 | async-start | bytes 2359296 | tf_op jit(solution)/shard_map/reduce_scatter | solution.py:83
Sparse Core Ops, SparseCore 0:
  9.9 26.1 all-gather.4
  38.0 23.4 all-gather.8
  63.1 80.7 all-gather.10
  145.2 79.0 all-gather.6
  238.1 34.1 reduce-scatter.4
  275.4 90.4 all-reduce.2
  369.7 40.1 reduce-scatter.2
where the time goes:
time: 422 us; the launch traced here: 421 us
  waiting for transfers between devices  348 us (82%)
  matrix products  39.9 us (9%)
  between operations  14.3 us (3%)
  blocking collectives  11 us (3%)
  local copies, waits for them, and re-layouts  5.33 us (1%)
    psum x1, waiting for transfers between devices, local(): lax.psum((grad_out_a, grad_in_b, rank_local), 'tok')  86.5 us
    all_gather x1, waiting for transfers between devices, local(): in_rows = lax.all_gather(frozen_in, 'tok', axis=0, tiled=True)  80.7 us
    all_gather x1, waiting for transfers between devices, local(): lax.all_gather(frozen_out, 'tok', axis=1, tiled=True)  69.7 us
    reduce_scatter x1, waiting for transfers between devices, local(): lax.psum_scatter(dx_term, 'hid', scatter_dimension=1, tiled=True)  41.8 us
    reduce_scatter x1, waiting for transfers between devices, local(): lax.psum_scatter(rank_terms, 'hid', scatter_dimension=1, tiled=True)  27.9 us
    all_gather x1, waiting for transfers between devices, local(): lax.all_gather(tokens, 'hid', axis=1, tiled=True)  23.7 us
    all_gather x1, waiting for transfers between devices, local(): lax.all_gather(cotangent, 'hid', axis=1, tiled=True)  15.1 us
    all_gather x1, blocking collectives, local(): in_a_full = lax.all_gather(input_adapter_first, 'hid', axis=0, tiled=True)  11 us
  transfers between devices with their start and end apart: 7, of which 7 were waited for; matrix products, arithmetic and copies ran while one was open for 7% of the time, Pallas kernels for 0%

commit v1 on v0

--- a/solution.py
+++ b/solution.py
@@ -1,3 +1,4 @@
+import functools
 import math
 import jax
 import jax.numpy as jnp
@@ -7,6 +8,27 @@
 ADAPTER_SCALE = 0.5
 GELU_K = 0.7978845608
 GELU_C = 0.044715
+
+
+def produce_patches(vals, mesh_name):
+    piece_now = lax.axis_size(mesh_name)
+    back = lax.axis_index(mesh_name)
+    v1, latest, w1 = (piece_now, back, vals.shape[1])
+    state_now = lax.dynamic_update_slice_in_dim(
+        jnp.zeros([to_i * v1 if k == 1 else to_i for k, to_i in enumerate(vals.shape)], vals.dtype),
+        vals,
+        latest * w1,
+        axis=1,
+    )
+    for k0 in range(1, v1):
+        vals = lax.ppermute(vals, mesh_name, [(k, (k + 1) % v1) for k in range(v1)])
+        state_now = lax.dynamic_update_slice_in_dim(
+            state_now, vals, (latest - k0) % v1 * w1, axis=1
+        )
+    return state_now
+
+
+convert_matrix = functools.partial(produce_patches, mesh_name="hid")
 
 
 def gelu_pair(pre_activation):
@@ -35,7 +57,7 @@
     rank_width = input_adapter_second.shape[0]
     gradient_scale = ADAPTER_SCALE / math.sqrt(device_local_rows * lax.axis_size("tok"))
     full_tokens, full_cotan = (
-        lax.all_gather(tokens, "hid", axis=1, tiled=True),
+        convert_matrix(tokens),
         lax.all_gather(cotangent, "hid", axis=1, tiled=True),
     )
     in_rows = lax.all_gather(frozen_in, "tok", axis=0, tiled=True)

time: 422 us -> 399 us (0.945)
  waiting for transfers between devices: 348 us -> 320 us
    ppermute x0 -> x7, waiting for transfers between devices: none -> 31.6 us  [produce_patches(): vals = lax.ppermute(vals, mesh_name, [(k, (k + 1) % v1) for k in range(v1)])]
    all_gather x1 -> x0, waiting for transfers between devices: 23.7 us -> none  [local(): lax.all_gather(tokens, 'hid', axis=1, tiled=True)]
    all_gather x1, waiting for transfers between devices: 15.1 us -> 0.01 us  [local(): lax.all_gather(cotangent, 'hid', axis=1, tiled=True)]
    all_gather x1, waiting for transfers between devices: 69.7 us -> 58.7 us  [local(): lax.all_gather(frozen_out, 'tok', axis=1, tiled=True)]
    all_gather x1, waiting for transfers between devices: 80.7 us -> 73.7 us  [local(): in_rows = lax.all_gather(frozen_in, 'tok', axis=0, tiled=True)]
  transfers between devices with their start and end apart: 7 -> 13, of which waited for: 7 -> 11; matrix products, arithmetic and copies ran while one was open for 7% -> 8% of each run, Pallas kernels for 0% -> 0%
where the time goes in v1:
time: 399 us
  waiting for transfers between devices  320 us (80%)
  matrix products  42.9 us (11%)
  between operations  14.4 us (4%)
  blocking collectives  11.1 us (3%)
  local copies, waits for them, and re-layouts  6.66 us (2%)
    psum x1, waiting for transfers between devices, local(): lax.psum((grad_out_a, grad_in_b, rank_local), 'tok')  86.5 us
    all_gather x1, waiting for transfers between devices, local(): in_rows = lax.all_gather(frozen_in, 'tok', axis=0, tiled=True)  73.7 us
    all_gather x1, waiting for transfers between devices, local(): lax.all_gather(frozen_out, 'tok', axis=1, tiled=True)  58.7 us
    reduce_scatter x1, waiting for transfers between devices, local(): lax.psum_scatter(dx_term, 'hid', scatter_dimension=1, tiled=True)  41.7 us
    ppermute x7, waiting for transfers between devices, produce_patches(): vals = lax.ppermute(vals, mesh_name, [(k, (k + 1) % v1) for k in range(v1)])  31.6 us
    reduce_scatter x1, waiting for transfers between devices, local(): lax.psum_scatter(rank_terms, 'hid', scatter_dimension=1, tiled=True)  25.7 us
    all_gather x1, blocking collectives, local(): in_a_full = lax.all_gather(input_adapter_first, 'hid', axis=0, tiled=True)  11.1 us
  transfers between devices with their start and end apart: 13, of which 11 were waited for; matrix products, arithmetic and copies ran while one was open for 8% of the time, Pallas kernels for 0%

profile of v1, /device:TPU:0, one launch (start us, length us, event | category | flops | bytes accessed | tf_op | source)
XLA Modules:
  0.0 398.8 jit_solution(3100576399033958593)
XLA Ops:
  7.2 0.0 copy-start
  7.2 0.0 all-gather.4.cloned.1.call-start
  7.2 0.7 all-gather.4.cloned.1.call-update
  7.9 0.0 all-gather.6.cloned.1.call-start
  8.0 0.7 all-gather.6.cloned.1.call-update
  8.7 0.0 all-gather.8.cloned.1.call-start
  8.7 0.7 all-gather.8.cloned.1.call-update
  9.4 0.0 reduce-scatter.5.cloned.1.call-start
  9.4 0.5 collective-permute-start
  10.0 5.7 %collective-permute-done = bf16[512,128]{1,0:T(8,128)(2,1)S(1)} collective-permute-done((bf16[512,128]{1,0:T(8,128)(2,1)}, bf16[512,128]{1,0:T(8,128)(2,1)S(1)}, u32[]{:S(2)}, u32[]{:S(2)}) %collective-permute-start) | collective-permute-done | bytes 131104 | tf_op jit(solution)/shard_map/ppermute | solution.py:24
  15.7 5.3 %collective-permute-done.1 = bf16[512,128]{1,0:T(8,128)(2,1)S(1)} collective-permute-done((bf16[512,128]{1,0:T(8,128)(2,1)S(1)}, bf16[512,128]{1,0:T(8,128)(2,1)S(1)}, u32[]{:S(2)}, u32[]{:S(2)}) %collective-permute-start.1) | collective-permute-done | bytes 131104 | tf_op jit(solution)/shard_map/ppermute | solution.py:24
  21.0 5.3 %collective-permute-done.2 = bf16[512,128]{1,0:T(8,128)(2,1)S(1)} collective-permute-done((bf16[512,128]{1,0:T(8,128)(2,1)S(1)}, bf16[512,128]{1,0:T(8,128)(2,1)S(1)}, u32[]{:S(2)}, u32[]{:S(2)}) %collective-permute-start.2) | collective-permute-done | bytes 131104 | tf_op jit(solution)/shard_map/ppermute | solution.py:24
  26.3 11.1 %all_gather.15 = bf16[1024,128]{1,0:T(8,128)(2,1)S(1)} all-gather(bf16[128,128]{1,0:T(8,128)(2,1)} %param.12), channel_id=1, replica_groups=mesh['tok'=4,'hid'=8] {'hid'}, dimensions={0}, use_global_device_ids=true | all-gather | bytes 294912 | tf_op jit(solution)/shard_map/all_gather | solution.py:64
  37.4 0.1 broadcast_in_dim.3
  37.6 0.9 constant_dynamic-update-slice_fusion.7
  38.6 0.4 collective-permute-start.4
  39.0 4.9 %collective-permute-done.4 = bf16[512,128]{1,0:T(8,128)(2,1)S(1)} collective-permute-done((bf16[512,128]{1,0:T(8,128)(2,1)S(1)}, bf16[512,128]{1,0:T(8,128)(2,1)S(1)}, u32[]{:S(2)}, u32[]{:S(2)}) %collective-permute-start.4) | collective-permute-done | bytes 131104 | tf_op jit(solution)/shard_map/ppermute | solution.py:24
  44.0 5.2 %collective-permute-done.5 = bf16[512,128]{1,0:T(8,128)(2,1)S(1)} collective-permute-done((bf16[512,128]{1,0:T(8,128)(2,1)S(1)}, bf16[512,128]{1,0:T(8,128)(2,1)S(1)}, u32[]{:S(2)}, u32[]{:S(2)}) %collective-permute-start.5) | collective-permute-done | bytes 131104 | tf_op jit(solution)/shard_map/ppermute | solution.py:24
  49.3 5.2 %collective-permute-done.6 = bf16[512,128]{1,0:T(8,128)(2,1)S(1)} collective-permute-done((bf16[512,128]{1,0:T(8,128)(2,1)S(1)}, bf16[512,128]{1,0:T(8,128)(2,1)S(1)}, u32[]{:S(2)}, u32[]{:S(2)}) %collective-permute-start.6) | collective-permute-done | bytes 131104 | tf_op jit(solution)/shard_map/ppermute | solution.py:24
  54.5 0.4 fusion.10
  55.0 3.7 fusion.11
  58.7 1.7 fusion.9
  60.4 58.7 %all-gather.6.cloned.1.call-done = bf16[2048,1024]{1,0:T(8,128)(2,1)} async-done(((bf16[2048,256]{1,0:T(8,128)(2,1)}), bf16[2048,1024]{1,0:T(8,128)(2,1)}) %all-gather.6.cloned.1.call-update) | async-done | bytes 4194320 | tf_op jit(solution)/shard_map/all_gather | solution.py:80
  119.1 6.9 %fusion.8 = f32[512,2048]{1,0:T(8,128)} fusion(bf16[512,1024]{1,0:T(8,128)(2,1)} %all-gather.4.cloned.1.call-done, bf16[2048,1024]{1,0:T(8,128)(2,1)} %all-gather.6.cloned.1.call-done), kind=kOutput, calls=%fused_computation.26 | convolution fusion | flops 2147483648 | bytes 9437184 | tf_op jit(solution)/shard_map/td,fd->tf/dot_general | solution.py:77
  125.9 73.7 %all-gather.8.cloned.1.call-done = bf16[1024,2048]{1,0:T(8,128)(2,1)} async-done(((bf16[256,2048]{1,0:T(8,128)(2,1)}), bf16[1024,2048]{1,0:T(8,128)(2,1)}) %all-gather.8.cloned.1.call-update) | async-done | bytes 4194320 | tf_op jit(solution)/shard_map/all_gather | solution.py:63
  199.6 7.0 %multiply_convert_fusion = (bf16[512,2048]{1,0:T(8,128)(2,1)S(1)}, f32[512,2048]{1,0:T(8,128)S(1)}) fusion(f32[512,2048]{1,0:T(8,128)} %fusion.11, bf16[512,1024]{1,0:T(8,128)(2,1)S(1)} %constant_dynamic-update-slice_fusion, bf16[1024,2048]{1,0:T(8,128)(2,1)} %all-gather.8.cloned.1.call-done), kind=kOutput, calls=%fused_computation.9 | convolution fusion | flops 2159017984 | bytes 15728640 | tf_op jit(solution)/shard_map/dot_general | solution.py:68
  206.6 4.9 %fusion.6 = bf16[512,2048]{1,0:T(8,128)(2,1)S(1)} fusion(f32[512,2048]{1,0:T(8,128)S(1)} %get-tuple-element.16, f32[512,2048]{1,0:T(8,128)S(1)} %copy-done.8, f32[512,128]{1,0:T(8,128)S(1)} %fusion.9, bf16[2048,128]{1,0:T(8,128)(2,1)S(1)} %copy-done.6), kind=kOutput, calls=%fused_computation.8 | convolution fusion | flops 1632632832 | bytes 11272192 | tf_op jit(solution)/shard_map/dot_general | solution.py:83
  211.5 0.7 fusion.13
  212.3 0.7 fusion.16
  212.9 0.7 fusion.14
  213.7 0.7 fusion.15
  214.3 1.0 pad_maximum_fusion
  215.4 0.0 reduce-scatter.5.cloned.1.call-update
  215.4 0.2 all-reduce.3.cloned.1.call-start
  215.6 3.7 convolution_multiply_fusion.1
  219.4 5.0 %convolution_multiply_fusion = f32[2048,128]{1,0:T(8,128)} fusion(bf16[512,2048]{1,0:T(8,128)(2,1)} %copy-done.3, f32[512,128]{1,0:T(8,128)} %copy-done.5), kind=kOutput, calls=%fused_computation.11 | convolution fusion | flops 1610874880 | bytes 3407872 | tf_op jit(solution)/shard_map/dot_general | solution.py:91
  224.3 25.7 %reduce-scatter.5.cloned.1.call-done = f32[256,128]{1,0:T(8,128)} async-done(((f32[256,1024]{1,0:T(8,128)}), f32[256,128]{1,0:T(8,128)}) %reduce-scatter.5.cloned.1.call-update) | async-done | bytes 131088 | tf_op jit(solution)/shard_map/reduce_scatter | solution.py:106
  250.0 0.0 all-reduce.3.cloned.1.call-update
  250.0 0.0 reduce-scatter.3.cloned.1.call-start
  250.1 4.5 %fusion.12 = f32[512,1024]{1,0:T(8,128)S(1)} fusion(bf16[512,2048]{1,0:T(8,128)(2,1)S(1)} %copy-done.2, bf16[1024,2048]{1,0:T(8,128)(2,1)} %all-gather.8.cloned.1.call-done), kind=kOutput, calls=%fused_computation.30 | convolution fusion | flops 2147483648 | bytes 8388608 | tf_op jit(solution)/shard_map/tf,df->td/dot_general | solution.py:90
  254.6 2.4 multiply_add_fusion.2
  257.0 0.0 reduce-scatter.3.cloned.1.call-update
  257.0 86.5 %all-reduce.3.cloned.1.call-done = (f32[256,128]{1,0:T(8,128)}, f32[128,2048]{1,0:T(8,128)}, f32[2048,128]{1,0:T(8,128)}) async-done(((f32[256,128]{1,0:T(8,128)}, f32[128,2048]{1,0:T(8,128)}, f32[2048,128]{1,0:T(8,128)}), (f32[256,128]{1,0:T(8,128)}, f32[128,2048]{1,0:T(8,128)}, f32[2048,128]{1,0:T(8,128)})) %all-reduce.3.cloned.1.call-update) | async-done | bytes 2228240 | tf_op jit(solution)/shard_map/psum | solution.py:108
  343.5 1.5 slice_multiply_fusion
  345.0 0.7 copy.13
  345.7 41.7 %reduce-scatter.3.cloned.1.call-done = f32[512,128]{1,0:T(8,128)} async-done(((f32[512,1024]{1,0:T(8,128)}), f32[512,128]{1,0:T(8,128)}) %reduce-scatter.3.cloned.1.call-update) | async-done | bytes 262160 | tf_op jit(solution)/shard_map/reduce_scatter | solution.py:105
  387.4 2.3 copy.25
  389.7 2.3 copy.26
  (31 shorter events, 0.3 us)
Async XLA Ops:
  7.2 47.8 %copy-start = (bf16[128,2048]{1,0:T(8,128)(2,1)S(1)}, bf16[128,2048]{1,0:T(8,128)(2,1)}, u32[]{:S(2)}) copy-start(bf16[128,2048]{1,0:T(8,128)(2,1)} %param.13) | copy-start | bytes 1572868
  7.2 51.5 %all-gather.4.cloned.1.call-start = ((), (), s32[]{:S(2)}) async-start(), calls=%async_computation.2 | async-start | bytes 1179648 | tf_op jit(solution)/shard_map/all_gather | solution.py:61
  7.9 111.2 %all-gather.6.cloned.1.call-start = ((), (), s32[]{:S(2)}) async-start(), calls=%async_computation.3 | async-start | bytes 5242880 | tf_op jit(solution)/shard_map/all_gather | solution.py:80
  8.7 190.9 %all-gather.8.cloned.1.call-start = ((), (), s32[]{:S(2)}) async-start(), calls=%async_computation.4 | async-start | bytes 5242880 | tf_op jit(solution)/shard_map/all_gather | solution.py:63
  9.4 240.6 %reduce-scatter.5.cloned.1.call-start = ((), (), s32[]{:S(2)}) async-start(), calls=%async_computation.6 | async-start | bytes 1179648 | tf_op jit(solution)/shard_map/reduce_scatter | solution.py:106
  9.4 6.3 %collective-permute-start = (bf16[512,128]{1,0:T(8,128)(2,1)}, bf16[512,128]{1,0:T(8,128)(2,1)S(1)}, u32[]{:S(2)}, u32[]{:S(2)}) collective-permute-start(bf16[512,128]{1,0:T(8,128)(2,1)} %param.8), channel_id=1, source_target_pairs={{0,1},{1,2},{2,3},{3,4},{4,5},{5,6},{6,7},{7,0},{8,9},{9,10},{10,1... | collective-permute-start | bytes 393224 | tf_op jit(solution)/shard_map/ppermute | solution.py:24
  15.7 5.3 %collective-permute-start.1 = (bf16[512,128]{1,0:T(8,128)(2,1)S(1)}, bf16[512,128]{1,0:T(8,128)(2,1)S(1)}, u32[]{:S(2)}, u32[]{:S(2)}) collective-permute-start(bf16[512,128]{1,0:T(8,128)(2,1)S(1)} %collective-permute-done), channel_id=1, source_target_pairs={{0,1},{1,2},{2,3},{3,4},{4,5},{5,6},{6,7},{7,0},{8,9},{9,10},{10,1... | collective-permute-start | bytes 393224 | tf_op jit(solution)/shard_map/ppermute | solution.py:24
  21.0 5.3 %collective-permute-start.2 = (bf16[512,128]{1,0:T(8,128)(2,1)S(1)}, bf16[512,128]{1,0:T(8,128)(2,1)S(1)}, u32[]{:S(2)}, u32[]{:S(2)}) collective-permute-start(bf16[512,128]{1,0:T(8,128)(2,1)S(1)} %collective-permute-done.1), channel_id=1, source_target_pairs={{0,1},{1,2},{2,3},{3,4},{4,5},{5,6},{6,7},{7,0},{8,9},{9,10},{10,1... | collective-permute-start | bytes 393224 | tf_op jit(solution)/shard_map/ppermute | solution.py:24
  26.3 12.2 %collective-permute-start.3 = (bf16[512,128]{1,0:T(8,128)(2,1)S(1)}, bf16[512,128]{1,0:T(8,128)(2,1)S(1)}, u32[]{:S(2)}, u32[]{:S(2)}) collective-permute-start(bf16[512,128]{1,0:T(8,128)(2,1)S(1)} %collective-permute-done.2), channel_id=1, source_target_pairs={{0,1},{1,2},{2,3},{3,4},{4,5},{5,6},{6,7},{7,0},{8,9},{9,10},{10,1... | collective-permute-start | bytes 393224 | tf_op jit(solution)/shard_map/ppermute | solution.py:24
  38.5 20.2 %copy-start.7 = (bf16[128,1024]{1,0:T(8,128)(2,1)S(1)}, bf16[128,1024]{1,0:T(8,128)(2,1)}, u32[]{:S(2)}) copy-start(bf16[128,1024]{1,0:T(8,128)(2,1)} %param.15) | copy-start | bytes 786436
  38.6 5.3 %collective-permute-start.4 = (bf16[512,128]{1,0:T(8,128)(2,1)S(1)}, bf16[512,128]{1,0:T(8,128)(2,1)S(1)}, u32[]{:S(2)}, u32[]{:S(2)}) collective-permute-start(bf16[512,128]{1,0:T(8,128)(2,1)S(1)} %collective-permute-done.3), channel_id=1, source_target_pairs={{0,1},{1,2},{2,3},{3,4},{4,5},{5,6},{6,7},{7,0},{8,9},{9,10},{10,1... | collective-permute-start | bytes 393224 | tf_op jit(solution)/shard_map/ppermute | solution.py:24
  43.9 5.3 %collective-permute-start.5 = (bf16[512,128]{1,0:T(8,128)(2,1)S(1)}, bf16[512,128]{1,0:T(8,128)(2,1)S(1)}, u32[]{:S(2)}, u32[]{:S(2)}) collective-permute-start(bf16[512,128]{1,0:T(8,128)(2,1)S(1)} %collective-permute-done.4), channel_id=1, source_target_pairs={{0,1},{1,2},{2,3},{3,4},{4,5},{5,6},{6,7},{7,0},{8,9},{9,10},{10,1... | collective-permute-start | bytes 393224 | tf_op jit(solution)/shard_map/ppermute | solution.py:24
  49.2 5.3 %collective-permute-start.6 = (bf16[512,128]{1,0:T(8,128)(2,1)S(1)}, bf16[512,128]{1,0:T(8,128)(2,1)S(1)}, u32[]{:S(2)}, u32[]{:S(2)}) collective-permute-start(bf16[512,128]{1,0:T(8,128)(2,1)S(1)} %collective-permute-done.5), channel_id=1, source_target_pairs={{0,1},{1,2},{2,3},{3,4},{4,5},{5,6},{6,7},{7,0},{8,9},{9,10},{10,1... | collective-permute-start | bytes 393224 | tf_op jit(solution)/shard_map/ppermute | solution.py:24
  60.4 146.2 %copy-start.5 = (f32[512,128]{1,0:T(8,128)}, f32[512,128]{1,0:T(8,128)S(1)}, u32[]{:S(2)}) copy-start(f32[512,128]{1,0:T(8,128)S(1)} %fusion.9) | copy-start | bytes 786436
  125.9 80.7 %copy-start.6 = (bf16[2048,128]{1,0:T(8,128)(2,1)S(1)}, bf16[2048,128]{1,0:T(8,128)(2,1)}, u32[]{:S(2)}) copy-start(bf16[2048,128]{1,0:T(8,128)(2,1)} %param.14) | copy-start | bytes 1572868
  199.6 7.0 %copy-start.8 = (f32[512,2048]{1,0:T(8,128)S(1)}, f32[512,2048]{1,0:T(8,128)}, u32[]{:S(2)}) copy-start(f32[512,2048]{1,0:T(8,128)} %fusion.8) | copy-start | bytes 12582916
  206.6 6.3 %copy-start.3 = (bf16[512,2048]{1,0:T(8,128)(2,1)}, bf16[512,2048]{1,0:T(8,128)(2,1)S(1)}, u32[]{:S(2)}) copy-start(bf16[512,2048]{1,0:T(8,128)(2,1)S(1)} %get-tuple-element.15) | copy-start | bytes 6291460
  211.5 2.8 copy-start.1
  211.5 2.1 copy-start.4
  215.4 34.7 %copy-start.2 = (bf16[512,2048]{1,0:T(8,128)(2,1)S(1)}, bf16[512,2048]{1,0:T(8,128)(2,1)}, u32[]{:S(2)}) copy-start(bf16[512,2048]{1,0:T(8,128)(2,1)} %copy-done.1) | copy-start | bytes 6291460
  215.4 128.1 %all-reduce.3.cloned.1.call-start = ((), (), s32[]{:S(2)}) async-start(), calls=%async_computation.7 | async-start | bytes 4456448 | tf_op jit(solution)/shard_map/psum | solution.py:108
  250.0 137.4 %reduce-scatter.3.cloned.1.call-start = ((), (), s32[]{:S(2)}) async-start(), calls=%async_computation.5 | async-start | bytes 2359296 | tf_op jit(solution)/shard_map/reduce_scatter | solution.py:105
Sparse Core Ops, SparseCore 0:
  9.9 27.2 all-gather.3
  38.7 80.3 all-gather.5
  120.6 78.9 all-gather.7
  215.5 34.4 reduce-scatter.4
  253.0 90.4 all-reduce.2
  347.2 40.1 reduce-scatter.2
